TPU v7x, 128 devices: a whole 4x4x4 slice. The times are simulated.
128 devices in a mesh: gx: 16 (over z, y), gy: 8 (over x, core).
Axes of the slice: x: 4, y: 4, z: 4, core: 2. Of those that a mesh axis runs over, the one named last changes fastest.
Arguments:
- cell_state: float32 [17, 128, 128, 256], P(None, 'gx', 'gy')
- evap_rate: float32 [8], replicated, may hold values from 0.05 to 0.5
- parcels: float32 [8, 2097152], P(None, ('gx', 'gy'))
- crossing: int32 [2, 131072], P(None, ('gx', 'gy')), may hold values from 0 to 16383, as said below
- conv_mass: float32 [8, 262144], P(None, ('gx', 'gy')), may hold values from 0.5 to 2
- conv_owner: int32 [262144, 1], P(('gx', 'gy')), may hold values from 0 to 127; in each aligned block of 2048 rows (0 to 2047, 2048 to 4095, ...) at most 32 rows name the same one
- conv_cell: int32 [262144], P(('gx', 'gy')), may hold values from 0 to 32767
Outputs:
- new_cells: float32 [14, 128, 128, 256], P(None, 'gx', 'gy')
- new_parcels: float32 [8, 2097152], P(None, ('gx', 'gy'))
Inputs may be any that keep to these rules, and one draw needn't show every extreme that they name: On each device the 2048 entries of crossing are distinct local parcel slots. `conv_owner`: the rows of one device name one owner at most 32 times.
All inputs are finite; a program needn't handle non-finite values.
Results may differ from a plain program's by a relative error of at most 0.0003.
Values sent between devices are 32-bit elements; how exact they have to be, the bound alone decides.
A program may use at most 64 MiB of HBM per device.

v0:
```python
import math

import jax
import jax.numpy as jnp
from jax import lax
from jax.sharding import PartitionSpec as P

SECTIONS = 8
SPECIES = 6


def padded_2(value, sides, width):
    for axis, dim in sides:
        size, length = (lax.axis_size(axis), value.shape[dim])
        up = [(i, (i + 1) % size) for i in range(size)]
        down = [(j, i) for i, j in up]
        last = lax.slice_in_dim(value, length - width, length, axis=dim)
        initial = lax.slice_in_dim(value, 0, width, axis=dim)
        before = lax.ppermute(last, axis, up)
        after = lax.ppermute(initial, axis, down)
        value = jnp.concatenate([before, value, after], axis=dim)
    return value


def advect_split(first_padded, second_padded, wall_normal):
    count = SECTIONS + SPECIES
    amount_first = first_padded[:count]
    courant_first = first_padded[count]
    face_x = 0.5 * (courant_first[:-1] + courant_first[1:])
    flux_x = (
        jnp.maximum(face_x, 0.0) * amount_first[:, :-1]
        + jnp.minimum(face_x, 0.0) * amount_first[:, 1:]
    )
    change_x = flux_x[:, 1:] - flux_x[:, :-1]
    amount_second = second_padded[:count]
    courant_second = second_padded[count]
    face_y = 0.5 * (courant_second[:, :-1] + courant_second[:, 1:])
    flux_y = (
        jnp.maximum(face_y, 0.0) * amount_second[:, :, :-1]
        + jnp.minimum(face_y, 0.0) * amount_second[:, :, 1:]
    )
    change_y = flux_y[:, :, 1:] - flux_y[:, :, :-1]
    center = amount_first[:, 1:-1]
    face_z = 0.5 * (wall_normal[:, :, :-1] + wall_normal[:, :, 1:])
    flux_z = (
        jnp.maximum(face_z, 0.0) * center[:, :, :, :-1]
        + jnp.minimum(face_z, 0.0) * center[:, :, :, 1:]
    )
    flux_z = jnp.pad(flux_z, ((0, 0), (0, 0), (0, 0), (1, 1)))
    change_z = flux_z[:, :, :, 1:] - flux_z[:, :, :, :-1]
    return center - change_x - change_y - change_z


def evaporate(moved, evap_rate):
    sections = moved[:SECTIONS]
    species = moved[SECTIONS:]
    vapour = species[0]
    loss = evap_rate[:, None, None, None] * sections / (1.0 + vapour)
    passed = jnp.concatenate([loss[1:], jnp.zeros_like(loss[:1])], axis=0)
    new_sections = sections - loss + 0.5 * passed
    new_fuel = vapour + loss[0] + 0.5 * jnp.sum(loss[1:], axis=0)
    new_species = jnp.concatenate([new_fuel[None], species[1:]], axis=0)
    return (new_sections, new_species)


def advance(parcels):
    position = parcels[0:3]
    velocity = parcels[3:6]
    diameter = parcels[6]
    warmth = parcels[7]
    factor = 0.8 / (1.0 + diameter * diameter)
    velocity_new = velocity * (1.0 - factor)
    position_new = position + 0.5 * (velocity + velocity_new)
    diameter_new = diameter * (1.0 - 0.05 * warmth)
    warmth_new = warmth + factor * (1.0 - warmth)
    return jnp.concatenate(
        [position_new, velocity_new, diameter_new[None], warmth_new[None]], axis=0
    )


def bucket_rows(values, owner, owner_total, capacity):
    width = values.shape[0]
    row_total = owner.shape[0]
    block = math.gcd(row_total, 512)
    blocks = row_total // block
    positions = jnp.arange(block, dtype=jnp.int32)
    lower = (positions[:, None] > positions[None, :]).astype(jnp.bfloat16)
    owner_ids = jnp.arange(owner_total, dtype=jnp.int32)
    slot_ids = jnp.arange(capacity, dtype=jnp.float32)
    value_blocks = values.reshape(width, blocks, block).transpose(1, 0, 2)
    owner_blocks = owner.reshape(blocks, block)

    def bucket_step(carry, item):
        counts, filled = carry
        value_block, owner_block = item
        onehot = (owner_block[:, None] == owner_ids[None, :]).astype(jnp.float32)
        before = jnp.dot(lower, onehot.astype(jnp.bfloat16), preferred_element_type=jnp.float32)
        rank = jnp.sum((before + counts[None, :]) * onehot, axis=1)
        slot_hot = (rank[:, None] == slot_ids[None, :]).astype(jnp.float32)
        spread = value_block[:, :, None] * onehot[None]
        placed = jnp.einsum("sro,rw->sow", spread, slot_hot, precision=lax.Precision.HIGHEST)
        return ((counts + jnp.sum(onehot, axis=0), filled + placed), None)

    start = (
        jnp.zeros((owner_total,), jnp.float32),
        jnp.zeros((width, owner_total, capacity), jnp.float32),
    )
    (counts, filled), unused = lax.scan(bucket_step, start, (value_blocks, owner_blocks))
    return filled


def deposit_rows(mass_flat, cell_flat, plane_cells, size_z):
    row_total = cell_flat.shape[0]
    block = math.gcd(row_total, 1024)
    blocks = row_total // block
    plane_ids = jnp.arange(plane_cells, dtype=jnp.int32)
    depth_ids = jnp.arange(size_z, dtype=jnp.int32)
    mass_blocks = mass_flat.reshape(SECTIONS, blocks, block).transpose(1, 0, 2)
    cell_blocks = cell_flat.reshape(blocks, block)

    def deposit_step(total, item):
        mass_block, cell_block = item
        plane_hot = (cell_block[:, None] // size_z == plane_ids[None, :]).astype(jnp.float32)
        depth_hot = (cell_block[:, None] % size_z == depth_ids[None, :]).astype(jnp.float32)
        spread = mass_block[:, :, None] * plane_hot[None]
        added = jnp.einsum("srh,rl->shl", spread, depth_hot, precision=lax.Precision.HIGHEST)
        return (total + added, None)

    total, unused = lax.scan(
        deposit_step,
        jnp.zeros((SECTIONS, plane_cells, size_z), jnp.float32),
        (mass_blocks, cell_blocks),
    )
    return total


def on_device(cell_state, evap_rate, parcels, crossing, conv_mass, conv_owner, conv_cell):
    count = SECTIONS + SPECIES
    wall_normal = cell_state[count + 2]
    padded = padded_2(cell_state, (("gx", 1), ("gy", 2)), 1)
    first_padded = padded[: count + 1, :, 1:-1]
    second_padded = jnp.concatenate(
        [padded[:count, 1:-1], padded[count + 1 : count + 2, 1:-1]], axis=0
    )
    moved = advect_split(first_padded, second_padded, wall_normal)
    new_sections, new_species = evaporate(moved, evap_rate)
    size_x = cell_state.shape[1]
    size_y = cell_state.shape[2]
    size_z = cell_state.shape[3]
    owner_total = lax.axis_size("gx") * lax.axis_size("gy")
    row_total = conv_owner.shape[0]
    capacity = 2 * row_total // owner_total
    carried = jnp.concatenate([conv_mass, conv_cell.astype(jnp.float32)[None]], axis=0)
    filled = bucket_rows(carried, conv_owner[:, 0], owner_total, capacity)
    mass_buffer = filled[:SECTIONS]
    cell_buffer = filled[SECTIONS:].astype(jnp.int32)
    mass_in, cell_in = (
        lax.all_to_all(mass_buffer, ("gx", "gy"), split_axis=1, concat_axis=1, tiled=True),
        lax.all_to_all(cell_buffer, ("gx", "gy"), split_axis=1, concat_axis=1, tiled=True),
    )
    mass_flat = mass_in.reshape(SECTIONS, -1)
    cell_flat = cell_in.reshape(-1)
    deposit = deposit_rows(mass_flat, cell_flat, size_x * size_y, size_z)
    deposit = deposit.reshape(SECTIONS, size_x, size_y, size_z)
    new_cells = jnp.concatenate([new_sections + deposit, new_species], axis=0)
    advanced = advance(parcels)
    attr_count = advanced.shape[0]
    slot_total = advanced.shape[1]
    upper_count = slot_total // 128
    cross_count = crossing.shape[1]
    slots = jnp.concatenate([crossing[1], crossing[0]], axis=0)
    upper_hot = (slots[:, None] // 128 == jnp.arange(upper_count, dtype=jnp.int32)[None, :]).astype(
        jnp.float32
    )
    lower_hot = (slots[:, None] % 128 == jnp.arange(128, dtype=jnp.int32)[None, :]).astype(
        jnp.float32
    )
    folded = advanced.reshape(attr_count, upper_count, 128)
    picked = jnp.einsum("ahl,kh->akl", folded, upper_hot, precision=lax.Precision.HIGHEST)
    gathered = jnp.sum(picked * lower_hot[None], axis=2)
    leaving = jnp.stack([gathered[:, :cross_count], gathered[:, cross_count:]], axis=1)
    arrived = padded_2(leaving, (("gx", 1),), 1)
    incoming = jnp.concatenate([arrived[:, 3], arrived[:, 0]], axis=1)
    spread = incoming[:, :, None] * lower_hot[None]
    placed = jnp.einsum("akl,kh->ahl", spread, upper_hot, precision=lax.Precision.HIGHEST)
    hit = jnp.einsum("kh,kl->hl", upper_hot, lower_hot, precision=lax.Precision.HIGHEST)
    new_parcels = (folded * (1.0 - hit)[None] + placed).reshape(attr_count, slot_total)
    return (new_cells, new_parcels)


def solution(mesh):
    in_specs = (
        P(None, "gx", "gy", None),
        P(),
        P(None, ("gx", "gy")),
        P(None, ("gx", "gy")),
        P(None, ("gx", "gy")),
        P(("gx", "gy"), None),
        P(("gx", "gy")),
    )
    out_specs = (P(None, "gx", "gy", None), P(None, ("gx", "gy")))
    return jax.shard_map(
        on_device, mesh=mesh, in_specs=in_specs, out_specs=out_specs, check_vma=False
    )
```

profile of v0, /device:TPU:0, one launch (start us, length us, event | category | flops | bytes accessed | tf_op | source)
XLA Modules:
  0.0 115.6 jit_solution(11212295875644378909)
XLA Ops:
  0.6 1.9 %fusion.79 = (f32[17,1,16,256]{3,2,1,0:T(8,128)}, f32[17,1,16,256]{3,2,1,0:T(8,128)}) fusion(f32[17,8,16,256]{3,2,1,0:T(8,128)} %param.11), kind=kLoop, calls=%fused_computation.141 | loop fusion | bytes 1114112 | tf_op jit(solution)/shard_map/slice | solution.py:18
  2.5 1.7 %collective-permute-start = (f32[17,1,16,256]{3,2,1,0:T(8,128)}, f32[17,1,16,256]{3,2,1,0:T(8,128)}, u32[]{:S(2)}, u32[]{:S(2)}) collective-permute-start(f32[17,1,16,256]{3,2,1,0:T(8,128)} %get-tuple-element.215), channel_id=1, source_target_pairs={{0,8},{8,16},{16,24},{24,32},{32,40},{40,48},{48,56},{56,64},{64,7... | collective-permute-start | bytes 835592 | tf_op jit(solution)/shard_map/ppermute | solution.py:19
  4.2 4.9 %collective-permute-start.1 = (f32[17,1,16,256]{3,2,1,0:T(8,128)}, f32[17,1,16,256]{3,2,1,0:T(8,128)}, u32[]{:S(2)}, u32[]{:S(2)}) collective-permute-start(f32[17,1,16,256]{3,2,1,0:T(8,128)} %get-tuple-element.214), channel_id=1, source_target_pairs={{8,0},{16,8},{24,16},{32,24},{40,32},{48,40},{56,48},{64,56},{72,6... | collective-permute-start | bytes 835592 | tf_op jit(solution)/shard_map/ppermute | solution.py:20
  9.7 1.3 %reduce.7 = s32[2048]{0:T(1024)S(1)} reduce(s32[2048,1]{0,1:T(1,128)} %param.16, s32[]{:T(128)} %broadcast.329), dimensions={1}, to_apply=%param.16.reduce_sub_computation.3 | reduce | bytes 16388 | tf_op args[5]
  12.6 8.9 %while.26 = (s32[]{:T(128)}, f32[128]{0:T(128)S(1)}, f32[9,128,32]{1,2,0:T(8,128)S(1)}, s32[4,512]{1,0:T(4,128)S(1)}, f32[4,9,512]{2,1,0:T(8,128)S(1)}, /*index=5*/s32[]{:T(128)}, s32[]{:T(128)}) while((s32[]{:T(128)}, f32[128]{0:T(128)S(1)}, f32[9,128,32]{1,2,0:T(8,128)S(1)}, s32[4,512]{1,0:T(4,128)S(1)}, ...), condition=%wide.region_3.4_spmd.clone, body=%wide.region_0.3_spmd.clone.sunk | while | flops 295591552 | bytes 1416288 | solution.py:108
  13.3 1.6 %fusion.104 = f32[9,128,32]{1,2,0:T(8,128)S(1)} fusion(f32[512,128]{1,0:T(8,128)S(1)} %copy.89, f32[9,512]{1,0:T(8,128)S(1)} %dynamic-slice_bitcast_fusion.2, f32[9,128,32]{1,2,0:T(8,128)S(1)} %get-tuple-element.311, pred[]{:T(512)S(6)} %compare.35, f32[512]{0:T(512)S(1)} %fusion.103), kind=kOutput, calls=%fused_computation.12.clone.1 | convolution fusion | flops 227172352 | bytes 577537 | tf_op jit(solution)/shard_map/while/body/eval_jaxpr/sro,rw->sow/dot_general | solution.py:101
  15.5 1.6 %fusion.104 = f32[9,128,32]{1,2,0:T(8,128)S(1)} fusion(f32[512,128]{1,0:T(8,128)S(1)} %copy.89, f32[9,512]{1,0:T(8,128)S(1)} %dynamic-slice_bitcast_fusion.2, f32[9,128,32]{1,2,0:T(8,128)S(1)} %get-tuple-element.311, pred[]{:T(512)S(6)} %compare.35, f32[512]{0:T(512)S(1)} %fusion.103), kind=kOutput, calls=%fused_computation.12.clone.1 | convolution fusion | flops 227172352 | bytes 577537 | tf_op jit(solution)/shard_map/while/body/eval_jaxpr/sro,rw->sow/dot_general | solution.py:101
  17.7 1.6 %fusion.104 = f32[9,128,32]{1,2,0:T(8,128)S(1)} fusion(f32[512,128]{1,0:T(8,128)S(1)} %copy.89, f32[9,512]{1,0:T(8,128)S(1)} %dynamic-slice_bitcast_fusion.2, f32[9,128,32]{1,2,0:T(8,128)S(1)} %get-tuple-element.311, pred[]{:T(512)S(6)} %compare.35, f32[512]{0:T(512)S(1)} %fusion.103), kind=kOutput, calls=%fused_computation.12.clone.1 | convolution fusion | flops 227172352 | bytes 577537 | tf_op jit(solution)/shard_map/while/body/eval_jaxpr/sro,rw->sow/dot_general | solution.py:101
  20.0 1.6 %fusion.104 = f32[9,128,32]{1,2,0:T(8,128)S(1)} fusion(f32[512,128]{1,0:T(8,128)S(1)} %copy.89, f32[9,512]{1,0:T(8,128)S(1)} %dynamic-slice_bitcast_fusion.2, f32[9,128,32]{1,2,0:T(8,128)S(1)} %get-tuple-element.311, pred[]{:T(512)S(6)} %compare.35, f32[512]{0:T(512)S(1)} %fusion.103), kind=kOutput, calls=%fused_computation.12.clone.1 | convolution fusion | flops 227172352 | bytes 577537 | tf_op jit(solution)/shard_map/while/body/eval_jaxpr/sro,rw->sow/dot_general | solution.py:101
  22.3 7.1 %all-to-all-start.1 = ((s32[1,128,32]{2,0,1:T(1,128)}), s32[1,128,32]{2,0,1:T(1,128)}, u32[]{:S(2)}, u32[]{:S(2)}) async-start(s32[1,128,32]{2,0,1:T(1,128)} %copy.62), calls=%async_computation.1 | async-start | bytes 131072 | tf_op jit(solution)/shard_map/all_to_all | solution.py:159
  32.9 3.9 %multiply_reduce_fusion = f32[2048,8]{0,1:T(8,128)S(1)} fusion(f32[2048,128]{0,1:T(8,128)S(1)} %fusion.61, f32[128,1024]{0,1:T(8,128)S(1)} %bitcast.101, s32[2048]{0:T(1024)S(1)} %get-tuple-element.232), kind=kOutput, calls=%fused_computation.50 | convolution fusion | flops 3225665536 | bytes 1646592
  37.4 5.1 %collective-permute-start.4 = (f32[8,1,1024]{2,0,1:T(8,128)}, f32[8,1,1024]{2,0,1:T(8,128)}, u32[]{:S(2)}, u32[]{:S(2)}) collective-permute-start(f32[8,1,1024]{2,0,1:T(8,128)} %get-tuple-element.230), channel_id=1, source_target_pairs={{8,0},{16,8},{24,16},{32,24},{40,32},{48,40},{56,48},{64,56},{72,6... | collective-permute-start | bytes 98312 | tf_op jit(solution)/shard_map/ppermute | solution.py:20
  42.5 2.3 %copy.60 = f32[9,128,32]{2,0,1:T(8,128)} copy(f32[9,128,32]{1,2,0:T(8,128)} %copy-done.6) | data formatting | bytes 294912 | tf_op jit(solution)/shard_map/while | solution.py:108
  44.9 1.9 %slice_bitcast_fusion.3 = f32[128,8,32]{2,1,0:T(8,128)} fusion(f32[9,128,32]{2,0,1:T(8,128)} %copy.60), kind=kLoop, calls=%fused_computation.144 | loop fusion | bytes 262144
  46.8 1.8 %multiply_add_fusion = f32[14,8,16,255]{3,2,1,0:T(8,128)} fusion(f32[17,8,16,256]{3,2,1,0:T(8,128)S(1)} %copy-done, f32[8,16,255]{2,1,0:T(8,128)S(1)} %get-tuple-element.229, f32[8,16,255]{2,1,0:T(8,128)S(1)} %get-tuple-element.228), kind=kLoop, calls=%fused_computation.70 | loop fusion | flops 1370880 | bytes 5744640 | tf_op jit(solution)/shard_map/add | solution.py:46
  48.6 1.0 convolution_subtract_fusion
  49.6 1.3 %copy.70 = f32[2048,128]{1,0:T(8,128)} copy(f32[2048,128]{0,1:T(8,128)S(1)} %fusion.61) | data formatting | bytes 2097152 | tf_op jit(solution)/shard_map/convert_element_type | solution.py:175
  50.9 1.9 %reshape.385 = f32[128,1,256]{2,1,0:T(1,128)} reshape(f32[128,8,32]{2,1,0:T(8,128)} %slice_bitcast_fusion.3) | data formatting | bytes 262144
  53.8 10.4 %all-to-all-start = ((f32[128,1,256]{2,1,0:T(1,128)}), f32[128,1,256]{2,1,0:T(1,128)}, u32[]{:S(2)}, u32[]{:S(2)}) async-start(f32[128,1,256]{2,1,0:T(1,128)} %reshape.385), calls=%async_computation | async-start | bytes 262144 | tf_op jit(solution)/shard_map/all_to_all | solution.py:158
  64.2 1.6 %reduce.8 = s32[128,32]{1,0:T(8,128)S(1)} reduce(s32[1,128,32]{2,0,1:T(1,128)} %all-to-all-done.1, s32[]{:T(128)} %broadcast.329), dimensions={0}, to_apply=%all_to_all.7.reduce_sub_computation.3 | reduce | bytes 32772 | tf_op jit(solution)/shard_map/all_to_all | solution.py:159
  66.8 10.3 %fusion.58 = f32[8,128,128]{1,2,0:T(8,128)S(1)} fusion(f32[2048,128]{1,0:T(8,128)} %copy.70, f32[8,2048]{1,0:T(8,128)S(1)} %pad_maximum_fusion.6, s32[2048]{0:T(1024)} %copy-done.7, f32[128,128]{0,1:T(8,128)S(1)} %copy.68, f32[1,128,128]{1,2,0:T(8,128)} %copy.67, f32[1,128,128]{1,2,0:T(8,128)S(1)} %copy.66, f32[3,128,128]{1,2,0:T(8,128)} %copy.65, ...), kind=kOutput, calls=%fused_computation.72 | convolution fusion | flops 3224240128 | bytes 2236416 | tf_op jit(solution)/shard_map/akl,kh->ahl/dot_general | solution.py:185
  77.3 1.1 copy.85
  78.9 1.8 %reduce.9 = f32[128,256]{1,0:T(8,128)S(1)} reduce(f32[128,1,256]{2,1,0:T(1,128)} %all-to-all-done, f32[]{:T(128)} %broadcast.334), dimensions={1}, to_apply=%all_to_all.6.reduce_sub_computation | reduce | bytes 262148 | tf_op jit(solution)/shard_map/all_to_all | solution.py:158
  81.3 17.7 %while.27 = (s32[]{:T(128)}, f32[8,128,256]{2,1,0:T(8,128)}, f32[4,8,1024]{2,0,1:T(4,128)S(1)}, s32[4,1024]{1,0:T(4,128)S(1)}, s32[]{:T(128)}, /*index=5*/s32[]{:T(128)}) while((s32[]{:T(128)}, f32[8,128,256]{2,1,0:T(8,128)}, f32[4,8,1024]{2,0,1:T(4,128)S(1)}, s32[4,1024]{1,0:T(4,128)S(1)}, s32[]{:T(128)}, ...), condition=%wide.region_5.6_spmd.clone, body=%wide.region_4.5_spmd.clone.sunk | while | flops 3223342080 | bytes 3338327 | solution.py:129
  81.7 3.3 %fusion.108 = f32[8,128,256]{2,1,0:T(8,128)} fusion(f32[1024,128]{0,1:T(8,128)S(1)} %fusion.107, f32[8,1024]{1,0:T(8,128)S(1)} %bitcast.98, f32[8,128,256]{2,1,0:T(8,128)} %get-tuple-element.330, s32[1024]{0:T(1024)S(1)} %get-tuple-element.301, pred[]{:T(512)S(6)} %compare.36), kind=kOutput, calls=%fused_computation.31.clone.1 | convolution fusion | flops 3223060480 | bytes 2658305 | tf_op jit(solution)/shard_map/while/body/eval_jaxpr/srh,rl->shl/dot_general | solution.py:126
  85.1 4.5 %fusion.108 = f32[8,128,256]{2,1,0:T(8,128)} fusion(f32[1024,128]{0,1:T(8,128)S(1)} %fusion.107, f32[8,1024]{1,0:T(8,128)S(1)} %bitcast.98, f32[8,128,256]{2,1,0:T(8,128)} %get-tuple-element.330, s32[1024]{0:T(1024)S(1)} %get-tuple-element.301, pred[]{:T(512)S(6)} %compare.36), kind=kOutput, calls=%fused_computation.31.clone.1 | convolution fusion | flops 3223060480 | bytes 2658305 | tf_op jit(solution)/shard_map/while/body/eval_jaxpr/srh,rl->shl/dot_general | solution.py:126
  89.8 4.5 %fusion.108 = f32[8,128,256]{2,1,0:T(8,128)} fusion(f32[1024,128]{0,1:T(8,128)S(1)} %fusion.107, f32[8,1024]{1,0:T(8,128)S(1)} %bitcast.98, f32[8,128,256]{2,1,0:T(8,128)} %get-tuple-element.330, s32[1024]{0:T(1024)S(1)} %get-tuple-element.301, pred[]{:T(512)S(6)} %compare.36), kind=kOutput, calls=%fused_computation.31.clone.1 | convolution fusion | flops 3223060480 | bytes 2658305 | tf_op jit(solution)/shard_map/while/body/eval_jaxpr/srh,rl->shl/dot_general | solution.py:126
  94.4 4.5 %fusion.108 = f32[8,128,256]{2,1,0:T(8,128)} fusion(f32[1024,128]{0,1:T(8,128)S(1)} %fusion.107, f32[8,1024]{1,0:T(8,128)S(1)} %bitcast.98, f32[8,128,256]{2,1,0:T(8,128)} %get-tuple-element.330, s32[1024]{0:T(1024)S(1)} %get-tuple-element.301, pred[]{:T(512)S(6)} %compare.36), kind=kOutput, calls=%fused_computation.31.clone.1 | convolution fusion | flops 3223060480 | bytes 2658305 | tf_op jit(solution)/shard_map/while/body/eval_jaxpr/srh,rl->shl/dot_general | solution.py:126
  102.2 2.9 %collective-permute-start.3 = (f32[17,10,1,256]{3,0,2,1:T(8,128)S(1)}, f32[17,10,1,256]{3,0,2,1:T(8,128)S(1)}, u32[]{:S(2)}, u32[]{:S(2)}) collective-permute-start(f32[17,10,1,256]{3,0,2,1:T(8,128)S(1)} %copy.52), channel_id=1, source_target_pairs={{1,0},{2,1},{3,2},{4,3},{5,4},{6,5},{7,6},{0,7},{9,8},{10,9},{11,1... | collective-permute-start | bytes 522248 | tf_op jit(solution)/shard_map/ppermute | solution.py:20
  105.8 3.3 %collective-permute-done.2 = f32[17,10,1,256]{3,0,2,1:T(8,128)S(1)} collective-permute-done((f32[17,10,1,256]{3,0,2,1:T(8,128)S(1)}, f32[17,10,1,256]{3,0,2,1:T(8,128)S(1)}, u32[]{:S(2)}, u32[]{:S(2)}) %collective-permute-start.2) | collective-permute-done | bytes 174112 | tf_op jit(solution)/shard_map/ppermute | solution.py:19
  111.2 1.3 %fusion.52 = f32[14,8,16,256]{3,2,1,0:T(8,128)S(1)} fusion(f32[14,8,16,255]{3,2,1,0:T(8,128)S(1)} %copy-done.1, f32[14,8,17,256]{3,2,1,0:T(8,128)S(1)} %fusion.48, f32[14,9,16,256]{3,2,1,0:T(8,128)S(1)} %fusion.50, f32[17,8,16,256]{3,2,1,0:T(8,128)S(1)} %copy-done), kind=kLoop, calls=%fused_computation.64 | loop fusion | flops 2752512 | bytes 12837888 | tf_op jit(solution)/shard_map/sub | solution.py:51
  114.1 1.4 %pad_maximum_fusion.2 = f32[14,8,16,256]{3,2,1,0:T(8,128)} fusion(f32[5,8,16,256]{3,2,1,0:T(8,128)S(1)} %slice.207, f32[1,8,16,256]{3,2,1,0:T(8,128)S(1)} %fusion.74, f32[8,8,16,256]{3,2,1,0:T(8,128)S(1)} %add_add_fusion), kind=kLoop, calls=%fused_computation.69 | loop fusion | flops 917504 | bytes 3670016 | tf_op jit(solution)/shard_map/concatenate | solution.py:165
  (131 shorter events, 20.4 us)
Async XLA Ops:
  2.5 96.4 %collective-permute-start = (f32[17,1,16,256]{3,2,1,0:T(8,128)}, f32[17,1,16,256]{3,2,1,0:T(8,128)}, u32[]{:S(2)}, u32[]{:S(2)}) collective-permute-start(f32[17,1,16,256]{3,2,1,0:T(8,128)} %get-tuple-element.215), channel_id=1, source_target_pairs={{0,8},{8,16},{16,24},{24,32},{32,40},{40,48},{48,56},{56,64},{64,7... | collective-permute-start | bytes 835592 | tf_op jit(solution)/shard_map/ppermute | solution.py:19
  4.2 96.7 %collective-permute-start.1 = (f32[17,1,16,256]{3,2,1,0:T(8,128)}, f32[17,1,16,256]{3,2,1,0:T(8,128)}, u32[]{:S(2)}, u32[]{:S(2)}) collective-permute-start(f32[17,1,16,256]{3,2,1,0:T(8,128)} %get-tuple-element.214), channel_id=1, source_target_pairs={{8,0},{16,8},{24,16},{32,24},{40,32},{48,40},{56,48},{64,56},{72,6... | collective-permute-start | bytes 835592 | tf_op jit(solution)/shard_map/ppermute | solution.py:20
  12.6 16.8 %copy-start.3 = (f32[8,16384]{1,0:T(8,128)S(1)}, f32[8,16384]{1,0:T(8,128)}, u32[]{:S(2)}) copy-start(f32[8,16384]{1,0:T(8,128)} %param.13) | copy-start | bytes 1572868
  21.5 8.3 %copy-start.6 = (f32[9,128,32]{1,2,0:T(8,128)}, f32[9,128,32]{1,2,0:T(8,128)S(1)}, u32[]{:S(2)}) copy-start(f32[9,128,32]{1,2,0:T(8,128)S(1)} %get-tuple-element.124) | copy-start | bytes 442372
  21.5 10.2 %copy-start.8 = (s32[2,1024]{1,0:T(2,128)S(1)}, s32[2,1024]{1,0:T(2,128)}, u32[]{:S(2)}) copy-start(s32[2,1024]{1,0:T(2,128)} %param.14) | copy-start | bytes 24580
  22.3 31.5 %all-to-all-start.1 = ((s32[1,128,32]{2,0,1:T(1,128)}), s32[1,128,32]{2,0,1:T(1,128)}, u32[]{:S(2)}, u32[]{:S(2)}) async-start(s32[1,128,32]{2,0,1:T(1,128)} %copy.62), calls=%async_computation.1 | async-start | bytes 131072 | tf_op jit(solution)/shard_map/all_to_all | solution.py:159
  29.9 6.9 %copy-start.4 = (f32[3,128,128]{1,2,0:T(8,128)}, f32[3,128,128]{1,2,0:T(8,128)S(1)}, u32[]{:S(2)}) copy-start(f32[3,128,128]{1,2,0:T(8,128)S(1)} %copy.64) | copy-start | bytes 589828
  30.7 11.8 %copy-start = (f32[17,8,16,256]{3,2,1,0:T(8,128)S(1)}, f32[17,8,16,256]{3,2,1,0:T(8,128)}, u32[]{:S(2)}) copy-start(f32[17,8,16,256]{3,2,1,0:T(8,128)} %param.11) | copy-start | bytes 6684676
  31.8 16.8 %copy-start.7 = (s32[2048]{0:T(1024)}, s32[2048]{0:T(1024)S(1)}, u32[]{:S(2)}) copy-start(s32[2048]{0:T(1024)S(1)} %get-tuple-element.232) | copy-start | bytes 24580
  37.4 28.5 %collective-permute-start.4 = (f32[8,1,1024]{2,0,1:T(8,128)}, f32[8,1,1024]{2,0,1:T(8,128)}, u32[]{:S(2)}, u32[]{:S(2)}) collective-permute-start(f32[8,1,1024]{2,0,1:T(8,128)} %get-tuple-element.230), channel_id=1, source_target_pairs={{8,0},{16,8},{24,16},{32,24},{40,32},{48,40},{56,48},{64,56},{72,6... | collective-permute-start | bytes 98312 | tf_op jit(solution)/shard_map/ppermute | solution.py:20
  42.5 23.5 %collective-permute-start.5 = (f32[8,1,1024]{2,0,1:T(8,128)}, f32[8,1,1024]{2,0,1:T(8,128)}, u32[]{:S(2)}, u32[]{:S(2)}) collective-permute-start(f32[8,1,1024]{2,0,1:T(8,128)} %get-tuple-element.231), channel_id=1, source_target_pairs={{0,8},{8,16},{16,24},{24,32},{32,40},{40,48},{48,56},{56,64},{64,7... | collective-permute-start | bytes 98312 | tf_op jit(solution)/shard_map/ppermute | solution.py:19
  48.5 18.2 %copy-start.5 = (f32[3,128,128]{1,2,0:T(8,128)S(1)}, f32[3,128,128]{1,2,0:T(8,128)}, u32[]{:S(2)}) copy-start(f32[3,128,128]{1,2,0:T(8,128)} %copy-done.4) | copy-start | bytes 589828
  53.8 24.6 %all-to-all-start = ((f32[128,1,256]{2,1,0:T(1,128)}), f32[128,1,256]{2,1,0:T(1,128)}, u32[]{:S(2)}, u32[]{:S(2)}) async-start(f32[128,1,256]{2,1,0:T(1,128)} %reshape.385), calls=%async_computation | async-start | bytes 262144 | tf_op jit(solution)/shard_map/all_to_all | solution.py:158
  102.2 6.8 %collective-permute-start.2 = (f32[17,10,1,256]{3,0,2,1:T(8,128)S(1)}, f32[17,10,1,256]{3,0,2,1:T(8,128)S(1)}, u32[]{:S(2)}, u32[]{:S(2)}) collective-permute-start(f32[17,10,1,256]{3,0,2,1:T(8,128)S(1)} %copy.51), channel_id=1, source_target_pairs={{0,1},{1,2},{2,3},{3,4},{4,5},{5,6},{6,7},{7,0},{8,9},{9,10},{10,1... | collective-permute-start | bytes 522248 | tf_op jit(solution)/shard_map/ppermute | solution.py:19
  102.2 7.0 %collective-permute-start.3 = (f32[17,10,1,256]{3,0,2,1:T(8,128)S(1)}, f32[17,10,1,256]{3,0,2,1:T(8,128)S(1)}, u32[]{:S(2)}, u32[]{:S(2)}) collective-permute-start(f32[17,10,1,256]{3,0,2,1:T(8,128)S(1)} %copy.52), channel_id=1, source_target_pairs={{1,0},{2,1},{3,2},{4,3},{5,4},{6,5},{7,6},{0,7},{9,8},{10,9},{11,1... | collective-permute-start | bytes 522248 | tf_op jit(solution)/shard_map/ppermute | solution.py:20
  109.7 1.5 %copy-start.1 = (f32[14,8,16,255]{3,2,1,0:T(8,128)S(1)}, f32[14,8,16,255]{3,2,1,0:T(8,128)}, u32[]{:S(2)}) copy-start(f32[14,8,16,255]{3,2,1,0:T(8,128)} %multiply_add_fusion) | copy-start | bytes 5483524
  111.2 1.3 %copy-start.9 = (f32[8]{0:T(128)S(1)}, f32[8]{0:T(128)}, u32[]{:S(2)}) copy-start(f32[8]{0:T(128)} %param.12) | copy-start | bytes 100
  112.5 1.2 %copy-start.2 = (f32[8,128,256]{2,1,0:T(8,128)S(1)}, f32[8,128,256]{2,1,0:T(8,128)}, u32[]{:S(2)}) copy-start(f32[8,128,256]{2,1,0:T(8,128)} %get-tuple-element.125) | copy-start | bytes 3145732
where the time goes:
time: 117 us; the launch traced here: 116 us
  matrix products  39.6 us (34%)
  starting transfers between devices  32.2 us (28%)
  local copies, waits for them, and re-layouts  22.7 us (19%)
  other arithmetic  16.1 us (14%)
  waiting for transfers between devices  3.29 us (3%)
    dot_general x4, matrix products, deposit_step(): jnp.einsum('srh,rl->shl', spread, depth_hot, precision=lax.Precision.HIGH...  16.8 us
    ppermute x3, starting transfers between devices, padded_2(): after = lax.ppermute(initial, axis, down)  12.9 us
    all_to_all x1, starting transfers between devices, on_device(): lax.all_to_all(mass_buffer, ('gx', 'gy'), split_axis=1, concat_axis=1, ti...  10.4 us
    dot_general x1, matrix products, on_device(): jnp.einsum('akl,kh->ahl', spread, upper_hot, precision=lax.Precision.HIGH...  10.3 us
    unnamed x26, local copies, waits for them, and re-layouts  8.46 us
    all_to_all x1, starting transfers between devices, on_device(): lax.all_to_all(cell_buffer, ('gx', 'gy'), split_axis=1, concat_axis=1, ti...  7.12 us
    dot_general x4, matrix products, bucket_step(): jnp.einsum('sro,rw->sow', spread, slot_hot, precision=lax.Precision.HIGHEST)  6.26 us
    unnamed x1, matrix products  3.89 us
  transfers between devices with their start and end apart: 8, of which 1 were waited for; matrix products, arithmetic and copies ran while one was open for 60% of the time, Pallas kernels for 0%

commit v1 on v0

v1 whole, which is shorter than its diff:
```python
import functools

import jax
import jax.numpy as jnp
from jax import lax
from jax.experimental import pallas as pl
from jax.experimental.pallas import tpu as pltpu
from jax.sharding import PartitionSpec as P

SECTIONS = 8
SPECIES = 6
AMOUNTS = SECTIONS + SPECIES
MESH = pl.DeviceIdType.MESH
F32 = jnp.float32
BF16 = jnp.bfloat16


def split(value):
    high = value.astype(BF16)
    low = (value - high.astype(F32)).astype(BF16)
    return high, low


def dot_nt(left, right):
    return lax.dot_general(left, right, (((1,), (1,)), ((), ())), preferred_element_type=F32)


def iota(shape, dim):
    return lax.broadcasted_iota(jnp.int32, shape, dim)


def step_kernel(
    n_gx, n_gy, cap,
    cell_hbm, evap, par_hbm, cross_hbm, mass_hbm, owner_hbm, landing_hbm,
    out_cells, out_par,
    cell, par, cross, mass, owner, landing,
    hot_owner, slot_vals, packed, packed_own, inbox_y, turned, inbox_x,
    rows_t, hot_plane, hot_depth, spread,
    edge_y, halo_x, halo_y, coef, moved,
    advanced, adv_split, hot_low, leaving, arriving, placing,
    load_sems, s1_send, s1_recv, s2_send, s2_recv, hx_send, hx_recv, hy_send, hy_recv, p_send, p_recv,
):
    gx = lax.axis_index("gx")
    gy = lax.axis_index("gy")
    next_x = lax.rem(gx + 1, n_gx)
    prev_x = lax.rem(gx + n_gx - 1, n_gx)
    next_y = lax.rem(gy + 1, n_gy)
    prev_y = lax.rem(gy + n_gy - 1, n_gy)
    owners = n_gx * n_gy
    rows = mass.shape[1]
    size_x, size_y, size_z = cell.shape[1:]

    loads = [
        pltpu.make_async_copy(src, dst, load_sems.at[i])
        for i, (src, dst) in enumerate((
            (owner_hbm, owner), (mass_hbm, mass), (landing_hbm, landing),
            (cell_hbm, cell), (cross_hbm, cross), (par_hbm, par),
        ))
    ]
    for load in loads:
        load.start()

    barrier = pltpu.get_barrier_semaphore()
    for shift in range(1, n_gx):
        pl.semaphore_signal(barrier, inc=1, device_id=(lax.rem(gx + shift, n_gx), gy), device_id_type=MESH)
    for shift in range(1, n_gy):
        pl.semaphore_signal(barrier, inc=1, device_id=(gx, lax.rem(gy + shift, n_gy)), device_id_type=MESH)

    loads[0].wait()
    loads[1].wait()
    loads[2].wait()
    own = owner[...]
    own = lax.rem(own, n_gy) * n_gx + lax.div(own, n_gy)
    block = 256
    upper = (iota((block, block), 0) < iota((block, block), 1)).astype(F32).astype(BF16)
    count = jnp.zeros((owners, 1), F32)
    for b in range(rows // block):
        at = slice(b * block, (b + 1) * block)
        hot = (iota((owners, block), 0) == own[:, at]).astype(F32)
        hot_b = hot.astype(BF16)
        hot_owner[:, at] = hot_b
        before = jnp.dot(hot_b, upper, preferred_element_type=F32) + count
        rank = jnp.sum(hot * before, axis=0, keepdims=True).astype(jnp.int32)
        count = before[:, block - 1:] + hot[:, block - 1:]
        hot_slot = (iota((cap, block), 0) == rank).astype(F32)
        for s in range(SECTIONS):
            row = mass[s:s + 1, at]
            high = row.astype(BF16).astype(F32)
            slot_vals[0, s * cap:(s + 1) * cap, at] = (hot_slot * high).astype(BF16)
            slot_vals[1, s * cap:(s + 1) * cap, at] = (hot_slot * (row - high)).astype(BF16)
        where_to = landing[:, at]
        depth = lax.rem(where_to, 256)
        slot_vals[0, SECTIONS * cap:(SECTIONS + 1) * cap, at] = (hot_slot * (where_to - depth).astype(F32)).astype(BF16)
        slot_vals[1, SECTIONS * cap:(SECTIONS + 1) * cap, at] = (hot_slot * depth.astype(F32)).astype(BF16)
        slot_vals[0, (SECTIONS + 1) * cap:, at] = jnp.zeros((3 * cap, block), BF16)
        slot_vals[1, (SECTIONS + 1) * cap:, at] = jnp.zeros((3 * cap, block), BF16)
    filled = dot_nt(hot_owner[...], slot_vals[0]) + dot_nt(hot_owner[...], slot_vals[1])
    packed[...] = filled.reshape(n_gy, n_gx, 12 * cap)

    loads[3].wait()
    for f in range(AMOUNTS + 1):
        src = f if f < AMOUNTS else AMOUNTS + 1
        edge_y[0, f] = cell[src, :, 0, :]
        edge_y[1, f] = cell[src, :, size_y - 1, :]

    pl.semaphore_wait(barrier, n_gx + n_gy - 2)

    first = []
    for shift in range(1, n_gy):
        to = lax.rem(gy + shift, n_gy)
        copy = pltpu.make_async_remote_copy(
            packed.at[to], inbox_y.at[gy], s1_send.at[to], s1_recv.at[gy],
            device_id=(gx, to), device_id_type=MESH)
        copy.start()
        first.append(copy)
    halos = []
    for side, plane, to in ((0, size_x - 1, next_x), (1, 0, prev_x)):
        copy = pltpu.make_async_remote_copy(
            cell.at[0:AMOUNTS + 1, plane], halo_x.at[side], hx_send.at[side], hx_recv.at[side],
            device_id=(to, gy), device_id_type=MESH)
        copy.start()
        halos.append(copy)
    for side, edge, to in ((0, 1, next_y), (1, 0, prev_y)):
        copy = pltpu.make_async_remote_copy(
            edge_y.at[edge], halo_y.at[side], hy_send.at[side], hy_recv.at[side],
            device_id=(gx, to), device_id_type=MESH)
        copy.start()
        halos.append(copy)
    inbox_y[gy] = packed[gy]

    loads[4].wait()
    loads[5].wait()
    wide = adv_split.shape[2]
    chunks = par.shape[1] // wide
    attr = iota((8, wide), 0)
    for h in range(chunks):
        at = slice(h * wide, (h + 1) * wide)
        now = par[:, at]
        diameter = now[6:7]
        warmth = now[7:8]
        factor = 0.8 / (1.0 + diameter * diameter)
        keep = 1.0 - factor
        velocity = pltpu.roll(now, 5, 0)
        position_new = now + 0.5 * (velocity + velocity * keep)
        value = jnp.where(
            attr < 3, position_new,
            jnp.where(attr < 6, now * keep,
                      jnp.where(attr < 7, now * (1.0 - 0.05 * warmth), now + factor * (1.0 - now))))
        advanced[:, at] = value
        high = value.astype(BF16)
        both = jnp.concatenate([high.astype(F32), value - high.astype(F32)], axis=0)
        adv_split[h] = both.astype(BF16)
    slots = jnp.concatenate([cross[0:1], cross[1:2]], axis=1)
    total = slots.shape[1]
    low = lax.rem(slots, wide)
    high_part = lax.div(slots, wide)
    part = 256
    for b in range(total // part):
        at = slice(b * part, (b + 1) * part)
        hot_low[:, at] = (iota((wide, part), 0) == low[:, at]).astype(F32).astype(BF16)
    for b in range(total // part):
        at = slice(b * part, (b + 1) * part)
        picked = jnp.dot(adv_split[...].reshape(chunks * 16, wide), hot_low[:, at], preferred_element_type=F32)
        gathered = jnp.zeros((8, part), F32)
        for h in range(chunks):
            one = picked[h * 16:h * 16 + 8] + picked[h * 16 + 8:h * 16 + 16]
            gathered = jnp.where(high_part[:, at] == h, one, gathered)
        half = total // 2
        leaving[b * part // half, :, (b * part) % half:(b * part) % half + part] = gathered
    crossing = []
    for side, to in ((0, next_x), (1, prev_x)):
        copy = pltpu.make_async_remote_copy(
            leaving.at[side], arriving.at[side], p_send.at[side], p_recv.at[side],
            device_id=(to, gy), device_id_type=MESH)
        copy.start()
        crossing.append(copy)

    for shift in range(1, n_gy):
        src = lax.rem(gy + n_gy - shift, n_gy)
        pltpu.make_async_remote_copy(
            packed.at[src], inbox_y.at[src], s1_send.at[src], s1_recv.at[src],
            device_id=(gx, src), device_id_type=MESH).wait_recv()
    for x in range(n_gx):
        turned[x] = inbox_y[:, x, :]
    second = []
    for shift in range(1, n_gx):
        to = lax.rem(gx + shift, n_gx)
        copy = pltpu.make_async_remote_copy(
            turned.at[to], inbox_x.at[gx], s2_send.at[to], s2_recv.at[gx],
            device_id=(to, gy), device_id_type=MESH)
        copy.start()
        second.append(copy)
    inbox_x[gx] = turned[gx]

    for copy in halos:
        copy.wait_recv()
    row_y = iota((size_y, size_z), 0)
    lane_z = iota((size_y, size_z), 1)
    courant_x, courant_y, courant_z = AMOUNTS, AMOUNTS + 1, AMOUNTS + 2

    def across_y(plane, low_row, high_row):
        before = jnp.where(row_y == 0, low_row, pltpu.roll(plane, 1, 0))
        after = jnp.where(row_y == size_y - 1, high_row, pltpu.roll(plane, size_y - 1, 0))
        return before, after

    for x in range(size_x):
        mid = cell[courant_x, x]
        left = halo_x[0, AMOUNTS] if x == 0 else cell[courant_x, x - 1]
        right = halo_x[1, AMOUNTS] if x == size_x - 1 else cell[courant_x, x + 1]
        lower = 0.5 * (left + mid)
        upper_face = 0.5 * (mid + right)
        center = 1.0 - jnp.maximum(upper_face, 0.0) + jnp.minimum(lower, 0.0)
        coef[1, x] = jnp.maximum(lower, 0.0)
        coef[2, x] = -jnp.minimum(upper_face, 0.0)
        mid = cell[courant_y, x]
        before, after = across_y(mid, halo_y[0, AMOUNTS, x:x + 1], halo_y[1, AMOUNTS, x:x + 1])
        lower = 0.5 * (before + mid)
        upper_face = 0.5 * (mid + after)
        center = center - jnp.maximum(upper_face, 0.0) + jnp.minimum(lower, 0.0)
        coef[3, x] = jnp.maximum(lower, 0.0)
        coef[4, x] = -jnp.minimum(upper_face, 0.0)
        mid = cell[courant_z, x]
        lower = jnp.where(lane_z == 0, 0.0, 0.5 * (pltpu.roll(mid, 1, 1) + mid))
        upper_face = jnp.where(lane_z == size_z - 1, 0.0, 0.5 * (mid + pltpu.roll(mid, size_z - 1, 1)))
        center = center - jnp.maximum(upper_face, 0.0) + jnp.minimum(lower, 0.0)
        coef[5, x] = jnp.maximum(lower, 0.0)
        coef[6, x] = -jnp.minimum(upper_face, 0.0)
        coef[0, x] = center

    def transport(f, unused):
        for x in range(size_x):
            mid = cell[f, x]
            left = halo_x[0, f] if x == 0 else cell[f, x - 1]
            right = halo_x[1, f] if x == size_x - 1 else cell[f, x + 1]
            before, after = across_y(mid, halo_y[0, f, x:x + 1], halo_y[1, f, x:x + 1])
            moved[f, x] = (
                coef[0, x] * mid
                + coef[1, x] * left + coef[2, x] * right
                + coef[3, x] * before + coef[4, x] * after
                + coef[5, x] * pltpu.roll(mid, 1, 1) + coef[6, x] * pltpu.roll(mid, size_z - 1, 1))
        return unused

    lax.fori_loop(0, AMOUNTS, transport, 0)

    def evaporate(x, unused):
        vapour = moved[SECTIONS, x]
        inverse = 1.0 / (1.0 + vapour)
        fuel = vapour
        previous = None
        for s in range(SECTIONS):
            dense = moved[s, x]
            loss = evap[s] * dense * inverse
            fuel = fuel + (loss if s == 0 else 0.5 * loss)
            if s > 0:
                out_cells[s - 1, x] = previous + 0.5 * loss
            previous = dense - loss
        out_cells[SECTIONS - 1, x] = previous
        out_cells[SECTIONS, x] = fuel
        for f in range(SECTIONS + 1, AMOUNTS):
            out_cells[f, x] = moved[f, x]
        return unused

    lax.fori_loop(0, size_x, evaporate, 0)

    for copy in crossing:
        copy.wait_recv()
    for b in range(total // part):
        at = slice(b * part, (b + 1) * part)
        half = total // 2
        value = arriving[b * part // half, :, (b * part) % half:(b * part) % half + part]
        high = value.astype(BF16).astype(F32)
        both = jnp.concatenate([high, value - high], axis=0)
        for h in range(chunks):
            placing[h * 16:(h + 1) * 16, at] = jnp.where(high_part[:, at] == h, both, 0.0).astype(BF16)
        placing[chunks * 16:, at] = (iota((chunks, part), 0) == high_part[:, at]).astype(F32).astype(BF16)
    placed = dot_nt(placing[...], hot_low[...])
    for h in range(chunks):
        at = slice(h * wide, (h + 1) * wide)
        hit = placed[chunks * 16 + h:chunks * 16 + h + 1] > 0.5
        value = placed[h * 16:h * 16 + 8] + placed[h * 16 + 8:h * 16 + 16]
        out_par[:, at] = jnp.where(hit, value, advanced[:, at])

    for shift in range(1, n_gx):
        src = lax.rem(gx + n_gx - shift, n_gx)
        pltpu.make_async_remote_copy(
            turned.at[src], inbox_x.at[src], s2_send.at[src], s2_recv.at[src],
            device_id=(src, gy), device_id_type=MESH).wait_recv()
    for part_at in range(3):
        at = slice(part_at * 128, (part_at + 1) * 128)
        rows_t[at, :] = inbox_x[:, :, at].reshape(owners, 128).T
    landed = rows_t[SECTIONS * cap:(SECTIONS + 1) * cap, :].astype(jnp.int32)
    depth = lax.rem(landed, size_z)
    plane = lax.div(landed, size_z)
    planes = size_x * size_y
    for w in range(cap):
        at = slice(w * owners, (w + 1) * owners)
        hot_plane[:, at] = (iota((planes, owners), 0) == plane[w:w + 1]).astype(F32).astype(BF16)
        hot_depth[:, at] = (iota((size_z, owners), 0) == depth[w:w + 1]).astype(F32).astype(BF16)

    def deposit(s, unused):
        values = rows_t[pl.ds(pl.multiple_of(s * cap, cap), cap), :]
        high = values.astype(BF16).astype(F32)
        low = values - high
        for w in range(cap):
            at = slice(w * owners, (w + 1) * owners)
            hot = hot_plane[:, at].reshape(planes // 16, 16, owners)
            one = jnp.broadcast_to(high[w:w + 1], (16, owners)).astype(BF16)
            spread[0:planes, at] = (hot * one[None]).reshape(planes, owners)
            one = jnp.broadcast_to(low[w:w + 1], (16, owners)).astype(BF16)
            spread[planes:, at] = (hot * one[None]).reshape(planes, owners)
        added = dot_nt(spread[...], hot_depth[...])
        added = added[:planes] + added[planes:]
        out_cells[s] = out_cells[s] + added.reshape(size_x, size_y, size_z)
        return unused

    lax.fori_loop(0, SECTIONS, deposit, 0)

    for copy in first + second + halos + crossing:
        copy.wait_send()


def on_device(cell_state, evap_rate, parcels, crossing, conv_mass, conv_owner, conv_cell, n_gx, n_gy):
    fields, size_x, size_y, size_z = cell_state.shape
    rows = conv_mass.shape[1]
    owners = n_gx * n_gy
    cap = 2 * rows // owners
    slots = parcels.shape[1]
    total = 2 * crossing.shape[1]
    wide = 512
    chunks = slots // wide
    planes = size_x * size_y
    lanes = 12 * cap
    any_spec = pl.BlockSpec(memory_space=pl.ANY)
    dma = pltpu.SemaphoreType.DMA
    vmem = pltpu.VMEM
    return pl.pallas_call(
        functools.partial(step_kernel, n_gx, n_gy, cap),
        out_shape=(
            jax.ShapeDtypeStruct((AMOUNTS, size_x, size_y, size_z), F32),
            jax.ShapeDtypeStruct(parcels.shape, F32),
        ),
        in_specs=[any_spec, pl.BlockSpec(memory_space=pltpu.SMEM)] + [any_spec] * 5,
        out_specs=(pl.BlockSpec(memory_space=pltpu.VMEM), pl.BlockSpec(memory_space=pltpu.VMEM)),
        scratch_shapes=[
            vmem(cell_state.shape, F32), vmem(parcels.shape, F32), vmem(crossing.shape, jnp.int32),
            vmem(conv_mass.shape, F32), vmem((1, rows), jnp.int32), vmem((1, rows), jnp.int32),
            vmem((owners, rows), BF16), vmem((2, lanes, rows), BF16),
            vmem((n_gy, n_gx, lanes), F32), vmem((n_gx, lanes), F32), vmem((n_gy, n_gx, lanes), F32),
            vmem((n_gx, n_gy, lanes), F32), vmem((n_gx, n_gy, lanes), F32),
            vmem((lanes, owners), F32), vmem((planes, cap * owners), BF16),
            vmem((size_z, cap * owners), BF16), vmem((2 * planes, cap * owners), BF16),
            vmem((2, AMOUNTS + 1, size_x, size_z), F32), vmem((2, AMOUNTS + 1, size_y, size_z), F32),
            vmem((2, AMOUNTS + 1, size_x, size_z), F32),
            vmem((7, size_x, size_y, size_z), F32), vmem((AMOUNTS, size_x, size_y, size_z), F32),
            vmem(parcels.shape, F32), vmem((chunks, 16, wide), BF16), vmem((wide, total), BF16),
            vmem((2, 8, total // 2), F32), vmem((2, 8, total // 2), F32), vmem((chunks * 17, total), BF16),
            dma((6,)), dma((n_gy,)), dma((n_gy,)), dma((n_gx,)), dma((n_gx,)),
            dma((2,)), dma((2,)), dma((2,)), dma((2,)), dma((2,)), dma((2,)),
        ],
        compiler_params=pltpu.CompilerParams(
            collective_id=0, has_side_effects=True, vmem_limit_bytes=60 << 20),
        name="spray_step",
    )(
        cell_state, evap_rate, parcels, crossing, conv_mass,
        conv_owner.reshape(1, rows), conv_cell.reshape(1, rows),
    )


def solution(mesh):
    in_specs = (
        P(None, "gx", "gy", None),
        P(),
        P(None, ("gx", "gy")),
        P(None, ("gx", "gy")),
        P(None, ("gx", "gy")),
        P(("gx", "gy"), None),
        P(("gx", "gy")),
    )
    out_specs = (P(None, "gx", "gy", None), P(None, ("gx", "gy")))
    return jax.shard_map(
        functools.partial(on_device, n_gx=mesh.shape["gx"], n_gy=mesh.shape["gy"]),
        mesh=mesh, in_specs=in_specs, out_specs=out_specs, check_vma=False,
    )
```

time: 117 us -> 36.8 us (0.31); the launches traced: 116 us -> 36.6 us
  matrix products: 39.6 us -> 0 us
  Pallas kernels: 0 us -> 32.2 us
  starting transfers between devices: 32.2 us -> 0 us
  local copies, waits for them, and re-layouts: 22.7 us -> 3.76 us
  other arithmetic: 16.1 us -> 0 us
  waiting for transfers between devices: 3.29 us -> 0 us
    dot_general x14 -> x0, matrix products: 35.7 us -> none  [the longest x4 16.8 us: deposit_step(): jnp.einsum('srh,rl->shl', spread, depth_hot, precision=lax.Precision.HIGH...]
    pallas_call x0 -> x1, Pallas kernels: none -> 32.2 us  [on_device(): pl.pallas_call(functools.partial(step_kernel, n_gx, n_gy, cap), out_shape...]
    all_to_all x2 -> x0, starting transfers between devices: 17.6 us -> none  [the longest x1 10.4 us: on_device(): lax.all_to_all(mass_buffer, ('gx', 'gy'), split_axis=1, concat_axis=1, ti...]
    ppermute x6 -> x0, starting transfers between devices: 14.6 us -> none  [the longest x3 12.9 us: padded_2(): after = lax.ppermute(initial, axis, down)]
    unnamed x26 -> x4, local copies, waits for them, and re-layouts: 8.46 us -> 3.76 us
    unnamed x1 -> x0, matrix products: 3.89 us -> none
    concatenate x7 -> x0, local copies, waits for them, and re-layouts: 3.7 us -> none  [the longest x2 1.91 us: padded_2(): value = jnp.concatenate([before, value, after], axis=dim)]
    all_to_all x2 -> x0, other arithmetic: 3.46 us -> none  [the longest x1 1.83 us: on_device(): lax.all_to_all(mass_buffer, ('gx', 'gy'), split_axis=1, concat_axis=1, ti...]
  transfers between devices with their start and end apart: 8 -> 0, of which waited for: 1 -> 0; matrix products, arithmetic and copies ran while one was open for 60% -> 0% of each run, Pallas kernels for 0% -> 0%
where the time goes in v1:
time: 36.8 us; the launch traced here: 36.6 us
  Pallas kernels  32.2 us (88%)
  local copies, waits for them, and re-layouts  3.76 us (10%)
  between operations  0.65 us (2%)
    pallas_call x1, Pallas kernels, on_device(): pl.pallas_call(functools.partial(step_kernel, n_gx, n_gy, cap), out_shape...  32.2 us
    unnamed x4, local copies, waits for them, and re-layouts  3.76 us

profile of v1, /device:TPU:0, one launch (start us, length us, event | category | flops | bytes accessed | tf_op | source)
XLA Modules:
  0.0 36.6 jit_solution(6119652684621517522)
XLA Ops:
  0.6 32.2 %spray_step.1 = (f32[14,8,16,256]{3,2,1,0:T(8,128)}, f32[8,16384]{1,0:T(8,128)}) custom-call(f32[17,8,16,256]{3,2,1,0:T(8,128)} %cell_hbm.1, f32[8]{0:T(128)} %evap.1, f32[8,16384]{1,0:T(8,128)} %par_hbm.1, s32[2,1024]{1,0:T(2,128)} %cross_hbm.1, f32[8,2048]{1,0:T(8,128)} %mass_hbm.1, s32[1,2048]{1,0:T(1,128)} %bitcast.2, s32[1,2048]{1,0:T(1,128)} %bitcast.3), custom_call_target="tpu_custom_call" | custom-call | tf_op jit(solution)/shard_map/spray_step/pallas_call | solution.py:336
  32.8 0.0 copy-start
  32.8 3.0 %copy.11 = f32[14,8,16,256]{3,2,1,0:T(8,128)} copy(f32[14,8,16,256]{3,2,1,0:T(8,128)} %get-tuple-element.4) | data formatting | bytes 3670016
  35.8 0.0 copy-done
  35.8 0.8 %copy.12 = f32[8,16384]{1,0:T(8,128)} copy(f32[8,16384]{1,0:T(8,128)S(1)} %copy-done) | data formatting | bytes 1048576
Async XLA Ops:
  32.8 3.0 %copy-start = (f32[8,16384]{1,0:T(8,128)S(1)}, f32[8,16384]{1,0:T(8,128)}, u32[]{:S(2)}) copy-start(f32[8,16384]{1,0:T(8,128)} %get-tuple-element.5) | copy-start | bytes 1572868

commit v2 on v1

--- a/solution.py
+++ b/solution.py
@@ -13,12 +13,7 @@
 MESH = pl.DeviceIdType.MESH
 F32 = jnp.float32
 BF16 = jnp.bfloat16
-
-
-def split(value):
-    high = value.astype(BF16)
-    low = (value - high.astype(F32)).astype(BF16)
-    return high, low
+F8 = jnp.float8_e4m3fn
 
 
 def dot_nt(left, right):
@@ -32,10 +27,9 @@
 def step_kernel(
     n_gx, n_gy, cap,
     cell_hbm, evap, par_hbm, cross_hbm, mass_hbm, owner_hbm, landing_hbm,
-    out_cells, out_par,
+    out_cells, out_par, out_rows,
     cell, par, cross, mass, owner, landing,
     hot_owner, slot_vals, packed, packed_own, inbox_y, turned, inbox_x,
-    rows_t, hot_plane, hot_depth, spread,
     edge_y, halo_x, halo_y, coef, moved,
     advanced, adv_split, hot_low, leaving, arriving, placing,
     load_sems, s1_send, s1_recv, s2_send, s2_recv, hx_send, hx_recv, hy_send, hy_recv, p_send, p_recv,
@@ -285,38 +279,57 @@
         pltpu.make_async_remote_copy(
             turned.at[src], inbox_x.at[src], s2_send.at[src], s2_recv.at[src],
             device_id=(src, gy), device_id_type=MESH).wait_recv()
-    for part_at in range(3):
-        at = slice(part_at * 128, (part_at + 1) * 128)
-        rows_t[at, :] = inbox_x[:, :, at].reshape(owners, 128).T
-    landed = rows_t[SECTIONS * cap:(SECTIONS + 1) * cap, :].astype(jnp.int32)
-    depth = lax.rem(landed, size_z)
-    plane = lax.div(landed, size_z)
+    out_rows[...] = inbox_x[...]
+    for copy in first + second + halos + crossing:
+        copy.wait_send()
+
+
+def deposit_kernel(
+    cap, landed, cells, parcels, out_cells, out_par,
+    sums, rows_t, hot_plane, hot_depth, spread, sems,
+):
+    lasting = [pltpu.make_async_copy(parcels, out_par, sems.at[AMOUNTS])]
+    for f in range(SECTIONS, AMOUNTS):
+        lasting.append(pltpu.make_async_copy(cells.at[f], out_cells.at[f], sems.at[f]))
+    for copy in lasting:
+        copy.start()
+    size_x, size_y, size_z = cells.shape[1:]
     planes = size_x * size_y
+    n_gx, n_gy = landed.shape[:2]
+    owners = n_gx * n_gy
+    for part in range(3):
+        at = slice(part * 128, (part + 1) * 128)
+        rows_t[at, :] = landed[:, :, at].reshape(owners, 128).T
+    plane = lax.div(rows_t[SECTIONS * cap:(SECTIONS + 1) * cap, :].astype(jnp.int32), size_z)
+    depth = lax.rem(landed[:, :, SECTIONS * cap:].reshape(owners, 4 * cap).astype(jnp.int32), size_z)
     for w in range(cap):
         at = slice(w * owners, (w + 1) * owners)
         hot_plane[:, at] = (iota((planes, owners), 0) == plane[w:w + 1]).astype(F32).astype(BF16)
-        hot_depth[:, at] = (iota((size_z, owners), 0) == depth[w:w + 1]).astype(F32).astype(BF16)
+        hot_depth[at, :] = (iota((owners, size_z), 1) == depth[:, w:w + 1]).astype(F32).astype(F8)
 
     def deposit(s, unused):
         values = rows_t[pl.ds(pl.multiple_of(s * cap, cap), cap), :]
-        high = values.astype(BF16).astype(F32)
-        low = values - high
+        first = values.astype(F8).astype(F32)
+        rest = (values - first) * 16.0
+        second = rest.astype(F8).astype(F32)
+        third = (rest - second) * 16.0
         for w in range(cap):
             at = slice(w * owners, (w + 1) * owners)
             hot = hot_plane[:, at].reshape(planes // 16, 16, owners)
-            one = jnp.broadcast_to(high[w:w + 1], (16, owners)).astype(BF16)
-            spread[0:planes, at] = (hot * one[None]).reshape(planes, owners)
-            one = jnp.broadcast_to(low[w:w + 1], (16, owners)).astype(BF16)
-            spread[planes:, at] = (hot * one[None]).reshape(planes, owners)
-        added = dot_nt(spread[...], hot_depth[...])
-        added = added[:planes] + added[planes:]
-        out_cells[s] = out_cells[s] + added.reshape(size_x, size_y, size_z)
+            for p, piece in enumerate((first, second, third)):
+                one = jnp.broadcast_to(piece[w:w + 1], (16, owners)).astype(BF16)
+                spread[p * planes:(p + 1) * planes, at] = (hot * one[None]).reshape(planes, owners).astype(F8)
+        added = jnp.dot(spread[...], hot_depth[...], preferred_element_type=F32)
+        added = added[:planes] + added[planes:2 * planes] * (1 / 16) + added[2 * planes:] * (1 / 256)
+        sums[s] = cells[s] + added.reshape(size_x, size_y, size_z)
+        pltpu.make_async_copy(sums.at[s], out_cells.at[s], sems.at[s]).start()
         return unused
 
     lax.fori_loop(0, SECTIONS, deposit, 0)
-
-    for copy in first + second + halos + crossing:
-        copy.wait_send()
+    for s in range(SECTIONS):
+        pltpu.make_async_copy(sums.at[s], out_cells.at[s], sems.at[s]).wait()
+    for copy in lasting:
+        copy.wait()
 
 
 def on_device(cell_state, evap_rate, parcels, crossing, conv_mass, conv_owner, conv_cell, n_gx, n_gy):
@@ -330,25 +343,25 @@
     chunks = slots // wide
     planes = size_x * size_y
     lanes = 12 * cap
-    any_spec = pl.BlockSpec(memory_space=pl.ANY)
+    any_spec = pl.BlockSpec(memory_space=pltpu.HBM)
     dma = pltpu.SemaphoreType.DMA
     vmem = pltpu.VMEM
-    return pl.pallas_call(
+    whole = pl.BlockSpec(memory_space=vmem)
+    cells, new_parcels, landed = pl.pallas_call(
         functools.partial(step_kernel, n_gx, n_gy, cap),
         out_shape=(
-            jax.ShapeDtypeStruct((AMOUNTS, size_x, size_y, size_z), F32),
-            jax.ShapeDtypeStruct(parcels.shape, F32),
+            vmem((AMOUNTS, size_x, size_y, size_z), F32),
+            vmem(parcels.shape, F32),
+            vmem((n_gx, n_gy, lanes), F32),
         ),
         in_specs=[any_spec, pl.BlockSpec(memory_space=pltpu.SMEM)] + [any_spec] * 5,
-        out_specs=(pl.BlockSpec(memory_space=pltpu.VMEM), pl.BlockSpec(memory_space=pltpu.VMEM)),
+        out_specs=(whole, whole, whole),
         scratch_shapes=[
             vmem(cell_state.shape, F32), vmem(parcels.shape, F32), vmem(crossing.shape, jnp.int32),
             vmem(conv_mass.shape, F32), vmem((1, rows), jnp.int32), vmem((1, rows), jnp.int32),
             vmem((owners, rows), BF16), vmem((2, lanes, rows), BF16),
             vmem((n_gy, n_gx, lanes), F32), vmem((n_gx, lanes), F32), vmem((n_gy, n_gx, lanes), F32),
             vmem((n_gx, n_gy, lanes), F32), vmem((n_gx, n_gy, lanes), F32),
-            vmem((lanes, owners), F32), vmem((planes, cap * owners), BF16),
-            vmem((size_z, cap * owners), BF16), vmem((2 * planes, cap * owners), BF16),
             vmem((2, AMOUNTS + 1, size_x, size_z), F32), vmem((2, AMOUNTS + 1, size_y, size_z), F32),
             vmem((2, AMOUNTS + 1, size_x, size_z), F32),
             vmem((7, size_x, size_y, size_z), F32), vmem((AMOUNTS, size_x, size_y, size_z), F32),
@@ -358,12 +371,28 @@
             dma((2,)), dma((2,)), dma((2,)), dma((2,)), dma((2,)), dma((2,)),
         ],
         compiler_params=pltpu.CompilerParams(
-            collective_id=0, has_side_effects=True, vmem_limit_bytes=60 << 20),
+            collective_id=0, has_side_effects=True, vmem_limit_bytes=61 << 20),
         name="spray_step",
     )(
         cell_state, evap_rate, parcels, crossing, conv_mass,
         conv_owner.reshape(1, rows), conv_cell.reshape(1, rows),
     )
+    return pl.pallas_call(
+        functools.partial(deposit_kernel, cap),
+        out_shape=(
+            jax.ShapeDtypeStruct((AMOUNTS, size_x, size_y, size_z), F32),
+            jax.ShapeDtypeStruct(parcels.shape, F32),
+        ),
+        in_specs=[whole] * 3,
+        out_specs=(any_spec, any_spec),
+        scratch_shapes=[
+            vmem((SECTIONS, size_x, size_y, size_z), F32), vmem((lanes, owners), F32),
+            vmem((planes, cap * owners), BF16), vmem((cap * owners, size_z), F8),
+            vmem((3 * planes, cap * owners), F8), dma((AMOUNTS + 1,)),
+        ],
+        compiler_params=pltpu.CompilerParams(vmem_limit_bytes=28 << 20),
+        name="deposit",
+    )(landed, cells, new_parcels)
 
 
 def solution(mesh):

time: 36.8 us -> 29.2 us (0.79)
  local copies, waits for them, and re-layouts: 3.76 us -> 0 us
  Pallas kernels: 32.2 us -> 28.5 us
    pallas_call x1, Pallas kernels: 32.2 us -> 22.1 us  [on_device(): pl.pallas_call(functools.partial(step_kernel, n_gx, n_gy, cap), out_shape...]
    pallas_call x0 -> x1, Pallas kernels: none -> 6.37 us  [on_device(): pl.pallas_call(functools.partial(deposit_kernel, cap), out_shape=(jax.Sha...]
    unnamed x4 -> x0, local copies, waits for them, and re-layouts: 3.76 us -> none
where the time goes in v2:
time: 29.2 us; the launch traced here: 29.1 us
  Pallas kernels  28.5 us (98%)
  between operations  0.64 us (2%)
    pallas_call x1, Pallas kernels, on_device(): pl.pallas_call(functools.partial(step_kernel, n_gx, n_gy, cap), out_shape...  22.1 us
    pallas_call x1, Pallas kernels, on_device(): pl.pallas_call(functools.partial(deposit_kernel, cap), out_shape=(jax.Sha...  6.37 us

profile of v2, /device:TPU:0, one launch (start us, length us, event | category | flops | bytes accessed | tf_op | source)
XLA Modules:
  0.0 29.1 jit_solution(17296570377010396820)
XLA Ops:
  0.6 22.1 %spray_step.1 = (f32[14,8,16,256]{3,2,1,0:T(8,128)S(1)}, f32[8,16384]{1,0:T(8,128)S(1)}, f32[16,8,384]{2,1,0:T(8,128)S(1)}) custom-call(f32[17,8,16,256]{3,2,1,0:T(8,128)} %cell_hbm.1, f32[8]{0:T(128)} %evap.1, f32[8,16384]{1,0:T(8,128)} %par_hbm.1, s32[2,1024]{1,0:T(2,128)} %cross_hbm.1, f32[8,2048]{1,0:T(8,128)} %mass_hbm.1, s32[1,2048]{1,0:T(1,128)} %bitcast.2, ...), custom_call_target="tpu_custom_call" | custom-call | tf_op jit(solution)/shard_map/spray_step/pallas_call | solution.py:350
  22.7 6.4 %deposit.1 = (f32[14,8,16,256]{3,2,1,0:T(8,128)}, f32[8,16384]{1,0:T(8,128)}) custom-call(f32[16,8,384]{2,1,0:T(8,128)S(1)} %get-tuple-element.5.landed, f32[14,8,16,256]{3,2,1,0:T(8,128)S(1)} %get-tuple-element.6.cells, f32[8,16384]{1,0:T(8,128)S(1)} %get-tuple-element.7.parcels), custom_call_target="tpu_custom_call" | custom-call | tf_op jit(solution)/shard_map/deposit/pallas_call | solution.py:380
